TPU v7x, 32 devices: a whole 2x2x4 slice. The times are simulated.
32 devices in a mesh: dp: 16 (over z, y, core), seq: 2 (over x).
Axes of the slice: x: 2, y: 2, z: 4, core: 2. Of those that a mesh axis runs over, the one named last changes fastest.
Arguments:
- hidden_in: bfloat16 [4096, 2048], P(('dp', 'seq')), may hold values from -6 to 6
- norm_gain: float32 [2048], replicated, may hold values from 0.5 to 1.5
- resid_grad: bfloat16 [4096, 2048], P(('dp', 'seq')), may hold values from -3 to 3
- key_output_gradient: bfloat16 [4096, 512], P('dp', 'seq'), may hold values from -6 to 6
- value_output_gradient: bfloat16 [4096, 512], P('dp', 'seq'), may hold values from -6 to 6
- key_matrix: bfloat16 [2048, 512], P(None, 'seq'), may hold values from -0.125 to 0.125
- value_matrix: bfloat16 [2048, 512], P(None, 'seq'), may hold values from -0.125 to 0.125
Outputs:
- input_grad: bfloat16 [4096, 2048], P(('dp', 'seq'))
- key_weight_grad: float32 [2048, 512], P('dp', 'seq')
- value_weight_grad: float32 [2048, 512], P('dp', 'seq')
- gain_grad: float32 [2048], replicated
All inputs are finite; a program needn't handle non-finite values.
Results may differ from a plain program's by a relative error of at most 0.0029.
Values may be sent and summed in bfloat16 or wider, within the bound.
No kernel may reach another device: no remote copies, remote signals or barrier semaphores. Data moves between devices by JAX's collectives and lax.ppermute only.
A program may use at most 64 MiB of HBM per device.

v0:
```python
import math
import jax
import jax.numpy as jnp
from jax import lax
from jax.sharding import PartitionSpec as P

EPSILON = 1e-05


def normalize(rows, norm_gain):
    widened = rows.astype(jnp.float32)
    inv_rms = lax.rsqrt(jnp.mean(widened * widened, axis=-1, keepdims=True) + EPSILON)
    unit_rows = widened * inv_rms
    return (inv_rms, unit_rows, (unit_rows * norm_gain).astype(jnp.bfloat16))


def per_device(
    hidden_in,
    norm_gain,
    resid_grad,
    key_output_gradient,
    value_output_gradient,
    key_matrix,
    value_matrix,
):
    model_width = hidden_in.shape[1]
    pair_width = key_matrix.shape[1]
    total_tokens = key_output_gradient.shape[0] * lax.axis_size("dp")
    scale = 1.0 / math.sqrt(total_tokens)
    inv_rms, unit_rows, normed = normalize(hidden_in, norm_gain)
    normed_piece = lax.all_gather(normed, "seq", axis=0, tiled=True)
    key_next = jnp.einsum(
        "td,tc->dc", normed_piece, key_output_gradient, preferred_element_type=jnp.float32
    )
    value_next = jnp.einsum(
        "td,tc->dc", normed_piece, value_output_gradient, preferred_element_type=jnp.float32
    )
    key_sum, value_sum = (
        lax.psum_scatter(key_next, "dp", scatter_dimension=0, tiled=True),
        lax.psum_scatter(value_next, "dp", scatter_dimension=0, tiled=True),
    )
    key_tok, value_tok = (
        lax.all_to_all(key_output_gradient, "seq", split_axis=0, concat_axis=1, tiled=True),
        lax.all_to_all(value_output_gradient, "seq", split_axis=0, concat_axis=1, tiled=True),
    )
    block_width = 2 * pair_width
    joined = jnp.concatenate([key_matrix, value_matrix], axis=1)
    piece = lax.all_gather(joined, "seq", axis=1, tiled=True)
    shards = piece.shape[1] // block_width
    blocks = piece.reshape(model_width, shards, block_width)
    key_piece = blocks[:, :, :pair_width].reshape(model_width, shards * pair_width)
    value_piece = blocks[:, :, pair_width:].reshape(model_width, shards * pair_width)
    key_term = jnp.einsum("tc,dc->td", key_tok, key_piece, preferred_element_type=jnp.float32)
    value_term = jnp.einsum("tc,dc->td", value_tok, value_piece, preferred_element_type=jnp.float32)
    normed_grad = key_term + value_term
    gain_total = lax.psum(jnp.sum(normed_grad * unit_rows, axis=0), ("dp", "seq"))
    scaled = normed_grad * norm_gain
    inner = jnp.mean(scaled * unit_rows, axis=-1, keepdims=True)
    input_grad = (resid_grad.astype(jnp.float32) + inv_rms * (scaled - unit_rows * inner)).astype(
        jnp.bfloat16
    )
    return (input_grad, key_sum * scale, value_sum * scale, gain_total * scale)


def solution(mesh):
    return jax.shard_map(
        per_device,
        mesh=mesh,
        in_specs=(
            P(("dp", "seq"), None),
            P(),
            P(("dp", "seq"), None),
            P("dp", "seq"),
            P("dp", "seq"),
            P(None, "seq"),
            P(None, "seq"),
        ),
        out_specs=(P(("dp", "seq"), None), P("dp", "seq"), P("dp", "seq"), P()),
        check_vma=False,
    )
```

profile of v0, /device:TPU:0, one launch (start us, length us, event | category | flops | bytes accessed | tf_op | source)
XLA Modules:
  0.0 237.8 jit_solution(16305939122774915193)
XLA Ops:
  7.2 0.0 all-gather.3.cloned.1.call-start
  7.2 1.5 copy.16
  8.7 1.5 copy.17
  10.2 1.4 pad_maximum_fusion
  11.6 0.0 copy-start.1
  11.7 0.0 all-gather.3.cloned.1.call-update
  11.7 4.4 %all-to-all-start.1 = ((bf16[2,128,256]{2,1,0:T(8,128)(2,1)}), bf16[2,128,256]{2,1,0:T(8,128)(2,1)S(1)}, u32[]{:S(2)}, u32[]{:S(2)}) async-start(bf16[2,128,256]{2,1,0:T(8,128)(2,1)} %bitcast.4), calls=%async_computation.1 | async-start | bytes 262144 | tf_op jit(solution)/shard_map/all_to_all | solution.py:44
  16.1 0.0 copy-done.1
  16.1 0.3 copy.15
  16.3 0.0 copy-start.3
  16.3 0.3 fusion.15
  16.6 4.0 %all-to-all-done.1 = bf16[2,128,256]{2,1,0:T(8,128)(2,1)S(1)} async-done(((bf16[2,128,256]{2,1,0:T(8,128)(2,1)}), bf16[2,128,256]{2,1,0:T(8,128)(2,1)S(1)}, u32[]{:S(2)}, u32[]{:S(2)}) %all-to-all-start.1) | async-done | bytes 131104 | tf_op jit(solution)/shard_map/all_to_all | solution.py:44
  20.6 3.4 %all-to-all-start = ((bf16[2,128,256]{2,1,0:T(8,128)(2,1)}), bf16[2,128,256]{2,1,0:T(8,128)(2,1)S(1)}, u32[]{:S(2)}, u32[]{:S(2)}) async-start(bf16[2,128,256]{2,1,0:T(8,128)(2,1)} %bitcast.1), calls=%async_computation | async-start | bytes 262144 | tf_op jit(solution)/shard_map/all_to_all | solution.py:43
  24.0 0.0 all-gather.5.cloned.1.call-start
  24.1 48.3 %all-gather.3.cloned.1.call-done = bf16[2048,1024]{0,1:T(8,128)(2,1)} async-done(((bf16[2048,512]{0,1:T(8,128)(2,1)}), bf16[2048,1024]{0,1:T(8,128)(2,1)}) %all-gather.3.cloned.1.call-update) | async-done | bytes 4194320 | tf_op jit(solution)/shard_map/all_gather | solution.py:48
  72.4 2.3 convolution_bitcast_fusion
  74.7 0.0 all-to-all-done
  74.7 0.0 copy-done.3
  74.7 3.3 %fusion.14 = (f32[2048]{0:T(1024)S(1)}, f32[128]{0:T(128)S(1)}, bf16[128,2048]{0,1:T(8,128)(2,1)}, f32[128,2048]{0,1:T(8,128)S(1)}) fusion(bf16[128,2048]{0,1:T(8,128)(2,1)S(1)} %copy.15, f32[128]{0:T(128)S(1)} %add_rsqrt_fusion, f32[2048]{0:T(1024)S(1)} %copy-done.3, f32[2048,128]{1,0:T(8,128)S(1)} %convolution_bitcast_fusion, ...), kind=kOutput, calls=%fused_computation.19 | convolution fusion | flops 271054720 | bytes 5391360 | tf_op jit(solution)/shard_map/tc,dc->td/dot_general | solution.py:53
  78.0 0.0 all-gather.5.cloned.1.call-update
  78.0 0.0 reduce-scatter.5.cloned.1.call-start
  78.1 21.7 %all-gather.5.cloned.1.call-done = bf16[256,2048]{0,1:T(8,128)(2,1)} async-done(((bf16[128,2048]{0,1:T(8,128)(2,1)}), bf16[256,2048]{0,1:T(8,128)(2,1)}) %all-gather.5.cloned.1.call-update) | async-done | bytes 1048592 | tf_op jit(solution)/shard_map/all_gather | solution.py:31
  99.8 0.0 copy-start
  99.8 3.1 %fusion.19 = f32[2048,256]{1,0:T(8,128)} fusion(bf16[256,2048]{0,1:T(8,128)(2,1)} %all-gather.5.cloned.1.call-done, bf16[256,256]{1,0:T(8,128)(2,1)} %param.11), kind=kOutput, calls=%fused_computation.29 | convolution fusion | flops 268435456 | bytes 3276800 | tf_op jit(solution)/shard_map/td,tc->dc/dot_general | solution.py:35
  102.8 0.0 reduce-scatter.5.cloned.1.call-update
  102.9 0.0 copy-start.2
  102.9 0.0 reduce-scatter.3.cloned.1.call-start
  102.9 0.0 copy-done
  102.9 2.7 %fusion.18 = f32[2048,256]{1,0:T(8,128)} fusion(bf16[256,2048]{0,1:T(8,128)(2,1)S(1)} %copy-done, bf16[256,256]{1,0:T(8,128)(2,1)} %param.10), kind=kOutput, calls=%fused_computation.28 | convolution fusion | flops 268435456 | bytes 3276800 | tf_op jit(solution)/shard_map/td,tc->dc/dot_general | solution.py:32
  105.6 0.0 reduce-scatter.3.cloned.1.call-update
  105.7 0.0 copy-done.2
  105.7 0.3 copy.14
  106.0 0.4 fusion.12
  106.4 1.0 copy.20
  107.4 39.7 %psum.7 = f32[2048]{0:T(1024)S(1)} all-reduce(f32[2048]{0:T(1024)S(1)} %get-tuple-element.12), channel_id=1, replica_groups=mesh['dp'=16,'seq'=2] {'dp','seq'}, use_global_device_ids=true, to_apply=%region_5.0 | all-reduce | flops 2048 | bytes 16384 | tf_op jit(solution)/shard_map/psum | solution.py:56
  147.1 0.6 broadcast_multiply_fusion.2
  147.7 17.6 %reduce-scatter.5.cloned.1.call-done = f32[128,256]{1,0:T(8,128)} async-done(((f32[2048,256]{1,0:T(8,128)}), f32[128,256]{1,0:T(8,128)}) %reduce-scatter.5.cloned.1.call-update) | async-done | bytes 131088 | tf_op jit(solution)/shard_map/reduce_scatter | solution.py:40
  165.3 1.6 broadcast_multiply_fusion
  166.9 62.8 %reduce-scatter.3.cloned.1.call-done = f32[128,256]{1,0:T(8,128)} async-done(((f32[2048,256]{1,0:T(8,128)}), f32[128,256]{1,0:T(8,128)}) %reduce-scatter.3.cloned.1.call-update) | async-done | bytes 131088 | tf_op jit(solution)/shard_map/reduce_scatter | solution.py:39
  229.7 1.6 broadcast_multiply_fusion.1
  (2 shorter events, 0.0 us)
Async XLA Ops:
  7.2 65.2 %all-gather.3.cloned.1.call-start = ((), (), s32[]{:S(2)}) async-start(), calls=%async_computation.4 | async-start | bytes 6291456 | tf_op jit(solution)/shard_map/all_gather | solution.py:48
  11.6 4.4 %copy-start.1 = (bf16[128,2048]{1,0:T(8,128)(2,1)S(1)}, bf16[128,2048]{1,0:T(8,128)(2,1)}, u32[]{:S(2)}) copy-start(bf16[128,2048]{1,0:T(8,128)(2,1)} %param.7) | copy-start | bytes 1572868
  11.7 8.9 %all-to-all-start.1 = ((bf16[2,128,256]{2,1,0:T(8,128)(2,1)}), bf16[2,128,256]{2,1,0:T(8,128)(2,1)S(1)}, u32[]{:S(2)}, u32[]{:S(2)}) async-start(bf16[2,128,256]{2,1,0:T(8,128)(2,1)} %bitcast.4), calls=%async_computation.1 | async-start | bytes 262144 | tf_op jit(solution)/shard_map/all_to_all | solution.py:44
  16.3 58.4 %copy-start.3 = (f32[2048]{0:T(1024)S(1)}, f32[2048]{0:T(1024)}, u32[]{:S(2)}) copy-start(f32[2048]{0:T(1024)} %param.8) | copy-start | bytes 24580
  20.6 54.1 %all-to-all-start = ((bf16[2,128,256]{2,1,0:T(8,128)(2,1)}), bf16[2,128,256]{2,1,0:T(8,128)(2,1)S(1)}, u32[]{:S(2)}, u32[]{:S(2)}) async-start(bf16[2,128,256]{2,1,0:T(8,128)(2,1)} %bitcast.1), calls=%async_computation | async-start | bytes 262144 | tf_op jit(solution)/shard_map/all_to_all | solution.py:43
  24.0 75.7 %all-gather.5.cloned.1.call-start = ((), (), s32[]{:S(2)}) async-start(), calls=%async_computation.5 | async-start | bytes 1572864 | tf_op jit(solution)/shard_map/all_gather | solution.py:31
  78.0 87.3 %reduce-scatter.5.cloned.1.call-start = ((), (), s32[]{:S(2)}) async-start(), calls=%async_computation.7 | async-start | bytes 2228224 | tf_op jit(solution)/shard_map/reduce_scatter | solution.py:40
  99.8 3.2 %copy-start = (bf16[256,2048]{0,1:T(8,128)(2,1)S(1)}, bf16[256,2048]{0,1:T(8,128)(2,1)}, u32[]{:S(2)}) copy-start(bf16[256,2048]{0,1:T(8,128)(2,1)} %all-gather.5.cloned.1.call-done) | copy-start | bytes 3145732
  102.9 2.8 %copy-start.2 = (bf16[128,2048]{1,0:T(8,128)(2,1)S(1)}, bf16[128,2048]{1,0:T(8,128)(2,1)}, u32[]{:S(2)}) copy-start(bf16[128,2048]{1,0:T(8,128)(2,1)} %param.9) | copy-start | bytes 1572868
  102.9 126.8 %reduce-scatter.3.cloned.1.call-start = ((), (), s32[]{:S(2)}) async-start(), calls=%async_computation.6 | async-start | bytes 2228224 | tf_op jit(solution)/shard_map/reduce_scatter | solution.py:39
Sparse Core Ops, SparseCore 0:
  11.8 60.5 all-gather.2
  78.2 21.5 all-gather.4
  103.5 61.7 reduce-scatter.4
  168.9 60.7 reduce-scatter.2
where the time goes:
time: 238 us
  waiting for transfers between devices  154 us (65%)
  blocking collectives  39.7 us (17%)
  between operations  13.9 us (6%)
  matrix products  11.4 us (5%)
  starting transfers between devices  7.94 us (3%)
  other arithmetic  5.9 us (2%)
  local copies, waits for them, and re-layouts  4.55 us (2%)
    reduce_scatter x1, waiting for transfers between devices, per_device(): lax.psum_scatter(key_next, 'dp', scatter_dimension=0, tiled=True)  62.8 us
    all_gather x1, waiting for transfers between devices, per_device(): piece = lax.all_gather(joined, 'seq', axis=1, tiled=True)  48.3 us
    psum x1, blocking collectives, per_device(): lax.psum(jnp.sum(normed_grad * unit_rows, axis=0), ('dp', 'seq'))  39.7 us
    all_gather x1, waiting for transfers between devices, per_device(): normed_piece = lax.all_gather(normed, 'seq', axis=0, tiled=True)  21.7 us
    reduce_scatter x1, waiting for transfers between devices, per_device(): lax.psum_scatter(value_next, 'dp', scatter_dimension=0, tiled=True)  17.6 us
  transfers between devices with their start and end apart: 6, of which 5 were waited for; matrix products, arithmetic and copies ran while one was open for 4% of the time, Pallas kernels for 0%

commit v1 on v0

--- a/solution.py
+++ b/solution.py
@@ -5,6 +5,20 @@
 from jax.sharding import PartitionSpec as P
 
 EPSILON = 1e-05
+
+
+def deliver_sectors(slab_in):
+    mesh_name = "seq"
+    block_now = jax.lax.axis_size(mesh_name)
+    s_next, response = (block_now, jax.lax.axis_index(mesh_name))
+    tall, t_next = (slab_in, 1)
+    while t_next < s_next:
+        outer = jax.lax.ppermute(tall, mesh_name, [(q, q ^ t_next) for q in range(s_next)])
+        prior = jnp.concatenate([tall, outer], axis=0)
+        block_out = jnp.concatenate([outer, tall], axis=0)
+        tall = jnp.where(response & t_next == 0, prior, block_out)
+        t_next = 2 * t_next
+    return tall
 
 
 def normalize(rows, norm_gain):
@@ -28,7 +42,7 @@
     total_tokens = key_output_gradient.shape[0] * lax.axis_size("dp")
     scale = 1.0 / math.sqrt(total_tokens)
     inv_rms, unit_rows, normed = normalize(hidden_in, norm_gain)
-    normed_piece = lax.all_gather(normed, "seq", axis=0, tiled=True)
+    normed_piece = deliver_sectors(normed)
     key_next = jnp.einsum(
         "td,tc->dc", normed_piece, key_output_gradient, preferred_element_type=jnp.float32
     )

time: 238 us -> 230 us (0.966)
  waiting for transfers between devices: 154 us -> 145 us
    all_gather x1 -> x0, waiting for transfers between devices: 21.7 us -> none  [per_device(): normed_piece = lax.all_gather(normed, 'seq', axis=0, tiled=True)]
    ppermute x0 -> x1, waiting for transfers between devices: none -> 13.4 us  [deliver_sectors(): jax.lax.ppermute(tall, mesh_name, [(q, q ^ t_next) for q in range(s_next)])]
  transfers between devices with their start and end apart: 6 -> 6, of which waited for: 5 -> 5; matrix products, arithmetic and copies ran while one was open for 4% -> 5% of each run, Pallas kernels for 0% -> 0%
where the time goes in v1:
time: 230 us; the launch traced here: 229 us
  waiting for transfers between devices  145 us (63%)
  blocking collectives  40.1 us (17%)
  between operations  13.8 us (6%)
  matrix products  11.7 us (5%)
  starting transfers between devices  8.25 us (4%)
  other arithmetic  5.91 us (3%)
  local copies, waits for them, and re-layouts  4.79 us (2%)
    reduce_scatter x1, waiting for transfers between devices, per_device(): lax.psum_scatter(key_next, 'dp', scatter_dimension=0, tiled=True)  62.9 us
    all_gather x1, waiting for transfers between devices, per_device(): piece = lax.all_gather(joined, 'seq', axis=1, tiled=True)  48.3 us
    psum x1, blocking collectives, per_device(): lax.psum(jnp.sum(normed_grad * unit_rows, axis=0), ('dp', 'seq'))  40.1 us
    reduce_scatter x1, waiting for transfers between devices, per_device(): lax.psum_scatter(value_next, 'dp', scatter_dimension=0, tiled=True)  16.2 us
    ppermute x1, waiting for transfers between devices, deliver_sectors(): jax.lax.ppermute(tall, mesh_name, [(q, q ^ t_next) for q in range(s_next)])  13.4 us
    unnamed x13, local copies, waits for them, and re-layouts  4.79 us
  transfers between devices with their start and end apart: 6, of which 5 were waited for; matrix products, arithmetic and copies ran while one was open for 5% of the time, Pallas kernels for 0%

profile of v1, /device:TPU:0, one launch (start us, length us, event | category | flops | bytes accessed | tf_op | source)
XLA Modules:
  0.0 229.4 jit_solution(10486366977643657375)
XLA Ops:
  7.2 0.0 copy-start
  7.2 0.0 all-gather.2.cloned.1.call-start
  7.2 1.6 copy.16
  8.8 0.0 copy-done
  8.8 0.6 copy.17
  9.5 1.5 pad_maximum_fusion
  10.9 0.0 copy-start.1
  10.9 0.0 all-gather.2.cloned.1.call-update
  10.9 4.4 %all-to-all-start.1 = ((bf16[2,128,256]{2,1,0:T(8,128)(2,1)}), bf16[2,128,256]{2,1,0:T(8,128)(2,1)S(1)}, u32[]{:S(2)}, u32[]{:S(2)}) async-start(bf16[2,128,256]{2,1,0:T(8,128)(2,1)} %bitcast.4), calls=%async_computation.1 | async-start | bytes 262144 | tf_op jit(solution)/shard_map/all_to_all | solution.py:58
  15.3 0.0 copy-done.1
  15.3 0.3 copy.15
  15.6 0.0 copy-start.3
  15.6 0.3 fusion.15
  15.9 4.0 %all-to-all-done.1 = bf16[2,128,256]{2,1,0:T(8,128)(2,1)S(1)} async-done(((bf16[2,128,256]{2,1,0:T(8,128)(2,1)}), bf16[2,128,256]{2,1,0:T(8,128)(2,1)S(1)}, u32[]{:S(2)}, u32[]{:S(2)}) %all-to-all-start.1) | async-done | bytes 131104 | tf_op jit(solution)/shard_map/all_to_all | solution.py:58
  19.9 3.4 %all-to-all-start = ((bf16[2,128,256]{2,1,0:T(8,128)(2,1)}), bf16[2,128,256]{2,1,0:T(8,128)(2,1)S(1)}, u32[]{:S(2)}, u32[]{:S(2)}) async-start(bf16[2,128,256]{2,1,0:T(8,128)(2,1)} %bitcast.1), calls=%async_computation | async-start | bytes 262144 | tf_op jit(solution)/shard_map/all_to_all | solution.py:57
  23.3 0.0 reduce-scatter.5.cloned.1.call-start
  23.3 48.3 %all-gather.2.cloned.1.call-done = bf16[2048,1024]{0,1:T(8,128)(2,1)} async-done(((bf16[2048,512]{0,1:T(8,128)(2,1)}), bf16[2048,1024]{0,1:T(8,128)(2,1)}) %all-gather.2.cloned.1.call-update) | async-done | bytes 4194320 | tf_op jit(solution)/shard_map/all_gather | solution.py:62
  71.6 3.3 %convolution_bitcast_fusion = f32[2048,128]{1,0:T(8,128)} fusion(bf16[2048,2,512]{0,2,1:T(8,128)(2,1)} %bitcast.23, bf16[2,128,256]{2,1,0:T(8,128)(2,1)S(1)} %all-to-all-done.1), kind=kOutput, calls=%fused_computation | convolution fusion | flops 268435456 | bytes 3276800 | tf_op jit(solution)/shard_map/tc,dc->td/dot_general | solution.py:68
  74.9 0.0 all-to-all-done
  74.9 0.0 copy-done.3
  74.9 3.1 %fusion.14 = (f32[2048]{0:T(1024)S(1)}, f32[128]{0:T(128)S(1)}, bf16[128,2048]{0,1:T(8,128)(2,1)S(1)}, f32[128,2048]{0,1:T(8,128)S(1)}) fusion(bf16[128,2048]{0,1:T(8,128)(2,1)S(1)} %copy.15, f32[128]{0:T(128)S(1)} %add_rsqrt_fusion, f32[2048]{0:T(1024)S(1)} %copy-done.3, f32[2048,128]{1,0:T(8,128)} %convolution_bitcast_fusion, ...), kind=kOutput, calls=%fused_computation.19 | convolution fusion | flops 271054720 | bytes 5391360 | tf_op jit(solution)/shard_map/tc,dc->td/dot_general | solution.py:67
  78.0 0.4 collective-permute-start
  78.3 13.4 %collective-permute-done = bf16[128,2048]{0,1:T(8,128)(2,1)S(1)} collective-permute-done((bf16[128,2048]{0,1:T(8,128)(2,1)S(1)}, bf16[128,2048]{0,1:T(8,128)(2,1)S(1)}, u32[]{:S(2)}, u32[]{:S(2)}) %collective-permute-start) | collective-permute-done | bytes 524320 | tf_op jit(solution)/shard_map/ppermute | solution.py:16
  91.8 2.6 %fusion.16 = f32[2048,256]{1,0:T(8,128)} fusion(bf16[256,256]{1,0:T(8,128)(2,1)} %param.11, bf16[128,2048]{0,1:T(8,128)(2,1)S(1)} %collective-permute-done, bf16[128,2048]{0,1:T(8,128)(2,1)S(1)} %get-tuple-element.14, pred[]{:T(512)S(6)} %eq.3), kind=kOutput, calls=%fused_computation.22 | convolution fusion | flops 273154048 | bytes 3276801 | tf_op jit(solution)/shard_map/td,tc->dc/dot_general | solution.py:49
  94.4 0.0 reduce-scatter.5.cloned.1.call-update
  94.4 0.0 reduce-scatter.3.cloned.1.call-start
  94.5 2.7 %fusion.17 = f32[2048,256]{1,0:T(8,128)} fusion(bf16[256,256]{1,0:T(8,128)(2,1)} %param.10, bf16[128,2048]{0,1:T(8,128)(2,1)S(1)} %collective-permute-done, bf16[128,2048]{0,1:T(8,128)(2,1)S(1)} %get-tuple-element.14, pred[]{:T(512)S(6)} %eq.3), kind=kOutput, calls=%fused_computation.23 | convolution fusion | flops 273154048 | bytes 3276801 | tf_op jit(solution)/shard_map/td,tc->dc/dot_general | solution.py:46
  97.2 0.0 copy-start.2
  97.2 0.0 reduce-scatter.3.cloned.1.call-update
  97.2 1.0 copy-done.2
  98.2 0.3 copy.14
  98.5 0.4 fusion.12
  98.9 1.0 copy.20
  100.0 40.1 %psum.7 = f32[2048]{0:T(1024)S(1)} all-reduce(f32[2048]{0:T(1024)S(1)} %get-tuple-element.12), channel_id=1, replica_groups=mesh['dp'=16,'seq'=2] {'dp','seq'}, use_global_device_ids=true, to_apply=%region_5.6 | all-reduce | flops 2048 | bytes 16384 | tf_op jit(solution)/shard_map/psum | solution.py:70
  140.0 0.6 broadcast_multiply_fusion.2
  140.6 16.2 %reduce-scatter.5.cloned.1.call-done = f32[128,256]{1,0:T(8,128)} async-done(((f32[2048,256]{1,0:T(8,128)}), f32[128,256]{1,0:T(8,128)}) %reduce-scatter.5.cloned.1.call-update) | async-done | bytes 131088 | tf_op jit(solution)/shard_map/reduce_scatter | solution.py:54
  156.8 1.6 broadcast_multiply_fusion
  158.4 62.9 %reduce-scatter.3.cloned.1.call-done = f32[128,256]{1,0:T(8,128)} async-done(((f32[2048,256]{1,0:T(8,128)}), f32[128,256]{1,0:T(8,128)}) %reduce-scatter.3.cloned.1.call-update) | async-done | bytes 131088 | tf_op jit(solution)/shard_map/reduce_scatter | solution.py:53
  221.3 1.6 broadcast_multiply_fusion.1
  (2 shorter events, 0.0 us)
Async XLA Ops:
  7.2 1.6 copy-start
  7.2 64.4 %all-gather.2.cloned.1.call-start = ((), (), s32[]{:S(2)}) async-start(), calls=%async_computation.4 | async-start | bytes 6291456 | tf_op jit(solution)/shard_map/all_gather | solution.py:62
  10.9 4.4 %copy-start.1 = (bf16[128,2048]{1,0:T(8,128)(2,1)S(1)}, bf16[128,2048]{1,0:T(8,128)(2,1)}, u32[]{:S(2)}) copy-start(bf16[128,2048]{1,0:T(8,128)(2,1)} %param.7) | copy-start | bytes 1572868
  10.9 8.9 %all-to-all-start.1 = ((bf16[2,128,256]{2,1,0:T(8,128)(2,1)}), bf16[2,128,256]{2,1,0:T(8,128)(2,1)S(1)}, u32[]{:S(2)}, u32[]{:S(2)}) async-start(bf16[2,128,256]{2,1,0:T(8,128)(2,1)} %bitcast.4), calls=%async_computation.1 | async-start | bytes 262144 | tf_op jit(solution)/shard_map/all_to_all | solution.py:58
  15.6 59.3 %copy-start.3 = (f32[2048]{0:T(1024)S(1)}, f32[2048]{0:T(1024)}, u32[]{:S(2)}) copy-start(f32[2048]{0:T(1024)} %param.8) | copy-start | bytes 24580
  19.9 55.0 %all-to-all-start = ((bf16[2,128,256]{2,1,0:T(8,128)(2,1)}), bf16[2,128,256]{2,1,0:T(8,128)(2,1)S(1)}, u32[]{:S(2)}, u32[]{:S(2)}) async-start(bf16[2,128,256]{2,1,0:T(8,128)(2,1)} %bitcast.1), calls=%async_computation | async-start | bytes 262144 | tf_op jit(solution)/shard_map/all_to_all | solution.py:57
  23.3 133.5 %reduce-scatter.5.cloned.1.call-start = ((), (), s32[]{:S(2)}) async-start(), calls=%async_computation.6 | async-start | bytes 2228224 | tf_op jit(solution)/shard_map/reduce_scatter | solution.py:54
  78.0 13.8 %collective-permute-start = (bf16[128,2048]{0,1:T(8,128)(2,1)S(1)}, bf16[128,2048]{0,1:T(8,128)(2,1)S(1)}, u32[]{:S(2)}, u32[]{:S(2)}) collective-permute-start(bf16[128,2048]{0,1:T(8,128)(2,1)S(1)} %get-tuple-element.14), channel_id=1, source_target_pairs={{0,1},{1,0},{2,3},{3,2},{4,5},{5,4},{6,7},{7,6},{8,9},{9,8},{10,11... | collective-permute-start | bytes 1572872 | tf_op jit(solution)/shard_map/ppermute | solution.py:16
  94.4 126.8 %reduce-scatter.3.cloned.1.call-start = ((), (), s32[]{:S(2)}) async-start(), calls=%async_computation.5 | async-start | bytes 2228224 | tf_op jit(solution)/shard_map/reduce_scatter | solution.py:53
  97.2 1.0 copy-start.2
Sparse Core Ops, SparseCore 0:
  11.1 60.5 all-gather.1
  94.6 62.1 reduce-scatter.4
  160.5 60.6 reduce-scatter.2
